TPU v7x, 32 devices: a whole 2x2x4 slice. The times are simulated.
32 devices in a mesh: row: 8 (over y, x, core), col: 4 (over z).
Axes of the slice: x: 2, y: 2, z: 4, core: 2. Of those that a mesh axis runs over, the one named last changes fastest.
Arguments:
- ancestor_inverse: float32 [6144, 6144], P('row', 'col'), may hold values from -6 to 6
- factor: float32 [6144, 2560], P('row', 'col'), may hold values from -0.078125 to 0.078125
- diag_inverse: float32 [640, 2560], P('row', 'col'), may hold values from -6 to 6
- widths: int32 [4], replicated, may hold values from 384 to 640
- member: int32 [4, 6144], P(None, 'row'), may hold values 0 or 1
Outputs:
- offdiag: float32 [6144, 2560], P('row', 'col')
- diag_blocks: float32 [640, 2560], P('row', 'col')
All inputs are finite; a program needn't handle non-finite values. No bound on the sum of `member` on one device may be relied on, other than what follows from the above.
Results may differ from a plain program's by a relative error of at most 0.0001.
Values sent between devices are 32-bit elements; how exact they have to be, the bound alone decides.
A program may use at most 128 MiB of HBM per device.

v0:
```python
import jax
import jax.numpy as jnp
from jax import lax
from jax.sharding import PartitionSpec as P

W = 640
NODES = 4


def broadcast(block, axis, holder):
    block = jnp.where(lax.axis_index(axis) == holder, block, jnp.zeros_like(block))
    return lax.psum(block, axis)


def per_device(ancestor_inverse, factor, diag_inverse, widths, member):
    grid_rows = lax.axis_size("row")
    grid_cols = lax.axis_size("col")
    groups = grid_rows // grid_cols
    my_row = lax.axis_index("row")
    my_col = lax.axis_index("col")
    shard_cols = factor.shape[1]
    col_start = my_col * shard_cols
    global_cols = col_start + jnp.arange(shard_cols, dtype=jnp.int32)
    node_of = global_cols // W
    within = global_cols % W
    select = (node_of[:, None] == jnp.arange(NODES, dtype=jnp.int32)[None, :]).astype(jnp.float32)
    width_col = jnp.dot(select, widths.astype(jnp.float32), precision=lax.Precision.HIGHEST)
    col_keep = (within.astype(jnp.float32) < width_col).astype(jnp.float32)
    row_keep = jnp.dot(member.T.astype(jnp.float32), select.T, precision=lax.Precision.HIGHEST)
    mask = row_keep * col_keep[None, :]
    masked = factor * mask
    rows_full = lax.all_gather(masked, "col", axis=1, tiled=True)
    pieces = []
    for offset in range(groups):
        pieces.append(broadcast(rows_full, "row", my_col * groups + offset))
    cols_full = jnp.concatenate(pieces, axis=0)
    partial_product = jnp.dot(
        ancestor_inverse,
        cols_full,
        precision=lax.Precision.HIGHEST,
        preferred_element_type=jnp.float32,
    )
    product = lax.psum_scatter(partial_product, "col", scatter_dimension=1, tiled=True)
    offdiag = -product * mask
    node_start = col_start // W * W
    left = lax.dynamic_slice_in_dim(rows_full, node_start, W, 1)
    local_gram = lax.dot_general(
        left,
        product,
        (((0,), (0,)), ((), ())),
        precision=lax.Precision.HIGHEST,
        preferred_element_type=jnp.float32,
    )
    gram = lax.psum_scatter(local_gram, "row", scatter_dimension=0, tiled=True)
    diag_rows_count = diag_inverse.shape[0]
    local_rows = my_row * diag_rows_count + jnp.arange(diag_rows_count, dtype=jnp.int32)
    inside = (local_rows.astype(jnp.float32)[:, None] < width_col[None, :]).astype(jnp.float32)
    diag_blocks = (diag_inverse + gram) * inside * col_keep[None, :]
    return (offdiag, diag_blocks)


def solution(mesh):
    in_specs = (P("row", "col"), P("row", "col"), P("row", "col"), P(), P(None, "row"))
    out_specs = (P("row", "col"), P("row", "col"))
    return jax.shard_map(
        per_device, mesh=mesh, in_specs=in_specs, out_specs=out_specs, check_vma=False
    )
```

profile of v0, /device:TPU:0, one launch (start us, length us, event | category | flops | bytes accessed | tf_op | source)
XLA Modules:
  0.0 610.8 jit_solution(1386914071417419135)
XLA Ops:
  7.2 0.0 all-gather.2.cloned.1.call-start
  7.2 1.0 convolution_reduce_fusion
  8.3 0.0 copy-start.1
  8.3 2.8 copy.7
  11.1 0.0 copy-done.1
  11.1 3.8 bitcast_multiply_fusion.1
  15.0 0.0 all-gather.2.cloned.1.call-update
  15.0 0.0 all-reduce.3.cloned.1.call-start
  15.1 143.9 %all-gather.2.cloned.1.call-done = f32[768,2560]{0,1:T(8,128)} async-done(((f32[768,640]{0,1:T(8,128)}), f32[768,2560]{0,1:T(8,128)}) %all-gather.2.cloned.1.call-update) | async-done | bytes 7864336 | tf_op jit(solution)/shard_map/all_gather | solution.py:32
  158.9 9.7 %broadcast_select_fusion.1 = (f32[768,2560]{0,1:T(8,128)}, f32[768,2560]{0,1:T(8,128)}) fusion(f32[768,2560]{0,1:T(8,128)} %all-gather.2.cloned.1.call-done, pred[]{:T(512)S(6)} %eq.21, pred[]{:T(512)S(6)} %eq.25), kind=kLoop, calls=%fused_computation.6 | loop fusion | flops 3932160 | bytes 23592962 | tf_op jit(solution)/shard_map/jit(_where)/select_n | solution.py:11
  168.7 0.0 all-reduce.3.cloned.1.call-update
  168.7 0.0 reduce-scatter.3.cloned.1.call-start
  168.7 204.6 %all-reduce.3.cloned.1.call-done = (f32[768,2560]{0,1:T(8,128)}, f32[768,2560]{0,1:T(8,128)}) async-done(((f32[768,2560]{0,1:T(8,128)}, f32[768,2560]{0,1:T(8,128)}), (f32[768,2560]{0,1:T(8,128)}, f32[768,2560]{0,1:T(8,128)})) %all-reduce.3.cloned.1.call-update) | async-done | bytes 15728656 | tf_op jit(solution)/shard_map/psum | solution.py:12
  373.3 45.2 %fusion.4 = f32[768,2560]{0,1:T(8,128)} fusion(f32[768,1536]{1,0:T(8,128)} %param.5, f32[768,2560]{0,1:T(8,128)} %get-tuple-element.4, f32[768,2560]{0,1:T(8,128)} %get-tuple-element.5), kind=kOutput, calls=%fused_computation.4 | convolution fusion | flops 36242718720 | bytes 28311552 | tf_op jit(solution)/shard_map/dot_general | solution.py:37
  418.5 0.0 reduce-scatter.3.cloned.1.call-update
  418.5 0.0 reduce-scatter.5.cloned.1.call-start
  418.6 136.5 %reduce-scatter.3.cloned.1.call-done = f32[768,640]{0,1:T(8,128)} async-done(((f32[768,2560]{0,1:T(8,128)}), f32[768,640]{0,1:T(8,128)}) %reduce-scatter.3.cloned.1.call-update) | async-done | bytes 1966096 | tf_op jit(solution)/shard_map/reduce_scatter | solution.py:43
  555.0 8.2 %fusion.7 = f32[640,640]{1,0:T(8,128)} fusion(f32[768,640]{0,1:T(8,128)} %reduce-scatter.3.cloned.1.call-done, f32[768,2560]{0,1:T(8,128)} %all-gather.2.cloned.1.call-done, s32[]{:T(128)S(6)} %select_n.44), kind=kOutput, calls=%fused_computation.9 | convolution fusion | flops 3774873600 | bytes 5570564 | tf_op jit(solution)/shard_map/dot_general | solution.py:47
  563.2 0.0 reduce-scatter.5.cloned.1.call-update
  563.2 3.1 bitcast_multiply_fusion
  566.4 0.0 copy-start
  566.4 2.9 copy.8
  569.2 33.3 %reduce-scatter.5.cloned.1.call-done = f32[80,640]{1,0:T(8,128)} async-done(((f32[640,640]{1,0:T(8,128)}), f32[80,640]{1,0:T(8,128)}) %reduce-scatter.5.cloned.1.call-update) | async-done | bytes 204816 | tf_op jit(solution)/shard_map/reduce_scatter | solution.py:54
  602.6 0.0 copy-done
  602.6 1.7 select_multiply_fusion
  (3 shorter events, 0.0 us)
Async XLA Ops:
  7.2 151.8 %all-gather.2.cloned.1.call-start = ((), (), s32[]{:S(2)}) async-start(), calls=%async_computation.2 | async-start | bytes 9830400 | tf_op jit(solution)/shard_map/all_gather | solution.py:32
  8.3 2.8 copy-start.1
  15.0 358.3 %all-reduce.3.cloned.1.call-start = ((), (), s32[]{:S(2)}) async-start(), calls=%async_computation.5 | async-start | bytes 31457280 | tf_op jit(solution)/shard_map/psum | solution.py:12
  168.7 386.4 %reduce-scatter.3.cloned.1.call-start = ((), (), s32[]{:S(2)}) async-start(), calls=%async_computation.3 | async-start | bytes 9830400 | tf_op jit(solution)/shard_map/reduce_scatter | solution.py:43
  418.5 184.1 %reduce-scatter.5.cloned.1.call-start = ((), (), s32[]{:S(2)}) async-start(), calls=%async_computation.4 | async-start | bytes 1843200 | tf_op jit(solution)/shard_map/reduce_scatter | solution.py:54
  566.4 36.2 %copy-start = (f32[80,640]{1,0:T(8,128)S(1)}, f32[80,640]{1,0:T(8,128)}, u32[]{:S(2)}) copy-start(f32[80,640]{1,0:T(8,128)} %param.7) | copy-start | bytes 614404
Sparse Core Ops, SparseCore 0:
  15.1 143.7 all-gather.1
  168.8 204.4 all-reduce.2
  418.6 136.3 reduce-scatter.2
  563.3 39.1 reduce-scatter.4
where the time goes:
time: 611 us
  waiting for transfers between devices  518 us (85%)
  matrix products  58.2 us (10%)
  other arithmetic  14.6 us (2%)
  between operations  13.8 us (2%)
    psum x1, waiting for transfers between devices, broadcast(): return lax.psum(block, axis)  205 us
    all_gather x1, waiting for transfers between devices, per_device(): rows_full = lax.all_gather(masked, 'col', axis=1, tiled=True)  144 us
    reduce_scatter x1, waiting for transfers between devices, per_device(): lax.psum_scatter(partial_product, 'col', scatter_dimension=1, tiled=True)  136 us
    dot_general x1, matrix products, per_device(): jnp.dot(ancestor_inverse, cols_full, precision=lax.Precision.HIGHEST, pre...  45.2 us
    reduce_scatter x1, waiting for transfers between devices, per_device(): gram = lax.psum_scatter(local_gram, 'row', scatter_dimension=0, tiled=True)  33.3 us
  transfers between devices with their start and end apart: 4, of which 4 were waited for; matrix products, arithmetic and copies ran while one was open for 1% of the time, Pallas kernels for 0%

commit v1 on v0

--- a/solution.py
+++ b/solution.py
@@ -29,7 +29,12 @@
     row_keep = jnp.dot(member.T.astype(jnp.float32), select.T, precision=lax.Precision.HIGHEST)
     mask = row_keep * col_keep[None, :]
     masked = factor * mask
-    rows_full = lax.all_gather(masked, "col", axis=1, tiled=True)
+    ring = [masked]
+    for hop in range(3):
+        ring.append(lax.ppermute(ring[-1], "col", [(dev, (dev + 1) % 4) for dev in range(4)]))
+    rows_full = jnp.roll(
+        jnp.concatenate(ring[::-1], axis=1), (lax.axis_index("col") + 1) * ring[0].shape[1], axis=1
+    )
     pieces = []
     for offset in range(groups):
         pieces.append(broadcast(rows_full, "row", my_col * groups + offset))

time: 611 us -> 625 us (1.023)
  local copies, waits for them, and re-layouts: 5.71 us -> 24.6 us
  waiting for transfers between devices: 518 us -> 510 us
    all_gather x1 -> x0, waiting for transfers between devices: 144 us -> none  [per_device(): rows_full = lax.all_gather(masked, 'col', axis=1, tiled=True)]
    ppermute x0 -> x3, waiting for transfers between devices: none -> 136 us  [per_device(): lax.ppermute(ring[-1], 'col', [(dev, (dev + 1) % 4) for dev in range(4)])]
    unnamed x6 -> x17, local copies, waits for them, and re-layouts: 5.71 us -> 23.2 us
  transfers between devices with their start and end apart: 4 -> 6, of which waited for: 4 -> 6; matrix products, arithmetic and copies ran while one was open for 1% -> 1% of each run, Pallas kernels for 0% -> 0%
where the time goes in v1:
time: 625 us; the launch traced here: 624 us
  waiting for transfers between devices  510 us (82%)
  matrix products  58.3 us (9%)
  local copies, waits for them, and re-layouts  24.6 us (4%)
  other arithmetic  14.6 us (2%)
  between operations  13.8 us (2%)
    psum x1, waiting for transfers between devices, broadcast(): return lax.psum(block, axis)  204 us
    reduce_scatter x1, waiting for transfers between devices, per_device(): lax.psum_scatter(partial_product, 'col', scatter_dimension=1, tiled=True)  136 us
    ppermute x3, waiting for transfers between devices, per_device(): lax.ppermute(ring[-1], 'col', [(dev, (dev + 1) % 4) for dev in range(4)])  136 us
    dot_general x1, matrix products, per_device(): jnp.dot(ancestor_inverse, cols_full, precision=lax.Precision.HIGHEST, pre...  45.2 us
    reduce_scatter x1, waiting for transfers between devices, per_device(): gram = lax.psum_scatter(local_gram, 'row', scatter_dimension=0, tiled=True)  33.3 us
    unnamed x17, local copies, waits for them, and re-layouts  23.2 us
  transfers between devices with their start and end apart: 6, of which 6 were waited for; matrix products, arithmetic and copies ran while one was open for 1% of the time, Pallas kernels for 0%

profile of v1, /device:TPU:0, one launch (start us, length us, event | category | flops | bytes accessed | tf_op | source)
XLA Modules:
  0.0 624.4 jit_solution(3755249591331621308)
XLA Ops:
  7.2 0.0 all-reduce.3.cloned.1.call-start
  7.2 1.0 convolution_reduce_fusion
  8.3 2.8 copy.7
  11.1 3.8 bitcast_multiply_fusion.1
  15.0 3.1 collective-permute-start
  18.0 44.8 %collective-permute-done = f32[768,640]{0,1:T(8,128)S(1)} collective-permute-done((f32[768,640]{0,1:T(8,128)S(1)}, f32[768,640]{0,1:T(8,128)S(1)}, u32[]{:S(2)}, u32[]{:S(2)}) %collective-permute-start) | collective-permute-done | bytes 1966112 | tf_op jit(solution)/shard_map/ppermute | solution.py:34
  62.9 0.0 copy-start.1
  62.9 1.3 copy-done.1
  64.2 0.0 collective-permute-start.1
  64.2 45.9 %collective-permute-done.1 = f32[768,640]{0,1:T(8,128)} collective-permute-done((f32[768,640]{0,1:T(8,128)S(1)}, f32[768,640]{0,1:T(8,128)}, u32[]{:S(2)}, u32[]{:S(2)}) %collective-permute-start.1) | collective-permute-done | bytes 1966112 | tf_op jit(solution)/shard_map/ppermute | solution.py:34
  110.0 0.0 collective-permute-start.2
  110.0 0.0 copy-start.2
  110.1 45.2 %collective-permute-done.2 = f32[768,640]{0,1:T(8,128)} collective-permute-done((f32[768,640]{0,1:T(8,128)}, f32[768,640]{0,1:T(8,128)}, u32[]{:S(2)}, u32[]{:S(2)}) %collective-permute-start.2) | collective-permute-done | bytes 1966112 | tf_op jit(solution)/shard_map/ppermute | solution.py:34
  155.3 3.0 constant_dynamic-update-slice_fusion.7
  158.3 2.9 constant_dynamic-update-slice_fusion.6
  161.2 0.0 copy-done.2
  161.2 1.4 constant_dynamic-update-slice_fusion.5
  162.6 1.4 constant_dynamic-update-slice_fusion.4
  164.0 3.0 constant_dynamic-update-slice_fusion.3
  167.1 2.9 constant_dynamic-update-slice_fusion.2
  170.0 1.5 constant_dynamic-update-slice_fusion.1
  171.5 1.4 constant_dynamic-update-slice_fusion
  172.9 9.7 %dynamic-slice_select_fusion.1 = (f32[768,2560]{0,1:T(8,128)}, f32[768,2560]{0,1:T(8,128)}) fusion(f32[768,5120]{0,1:T(8,128)} %constant_dynamic-update-slice_fusion, s32[]{:T(128)S(6)} %select_n.57, pred[]{:T(512)S(6)} %eq.24, pred[]{:T(512)S(6)} %eq.28), kind=kLoop, calls=%fused_computation.5 | loop fusion | flops 3932160 | bytes 23592966 | tf_op jit(solution)/shard_map/jit(_where)/select_n | solution.py:11
  182.6 0.0 all-reduce.3.cloned.1.call-update
  182.7 0.0 reduce-scatter.3.cloned.1.call-start
  182.7 204.2 %all-reduce.3.cloned.1.call-done = (f32[768,2560]{0,1:T(8,128)}, f32[768,2560]{0,1:T(8,128)}) async-done(((f32[768,2560]{0,1:T(8,128)}, f32[768,2560]{0,1:T(8,128)}), (f32[768,2560]{0,1:T(8,128)}, f32[768,2560]{0,1:T(8,128)})) %all-reduce.3.cloned.1.call-update) | async-done | bytes 15728656 | tf_op jit(solution)/shard_map/psum | solution.py:12
  386.9 45.2 %fusion.4 = f32[768,2560]{0,1:T(8,128)} fusion(f32[768,1536]{1,0:T(8,128)} %param.5, f32[768,2560]{0,1:T(8,128)} %get-tuple-element.4, f32[768,2560]{0,1:T(8,128)} %get-tuple-element.5), kind=kOutput, calls=%fused_computation.6 | convolution fusion | flops 36242718720 | bytes 28311552 | tf_op jit(solution)/shard_map/dot_general | solution.py:42
  432.0 0.0 copy-start
  432.0 0.0 reduce-scatter.3.cloned.1.call-update
  432.1 0.2 reduce-scatter.5.cloned.1.call-start
  432.3 0.0 copy-start.3
  432.3 136.3 %reduce-scatter.3.cloned.1.call-done = f32[768,640]{0,1:T(8,128)} async-done(((f32[768,2560]{0,1:T(8,128)}), f32[768,640]{0,1:T(8,128)}) %reduce-scatter.3.cloned.1.call-update) | async-done | bytes 1966096 | tf_op jit(solution)/shard_map/reduce_scatter | solution.py:48
  568.6 8.2 %fusion.7 = f32[640,640]{1,0:T(8,128)} fusion(f32[768,640]{0,1:T(8,128)} %reduce-scatter.3.cloned.1.call-done, f32[768,5120]{0,1:T(8,128)} %constant_dynamic-update-slice_fusion, s32[]{:T(128)S(6)} %dynamic_slice.11), kind=kOutput, calls=%fused_computation.9 | convolution fusion | flops 3774873600 | bytes 5570564 | tf_op jit(solution)/shard_map/dot_general | solution.py:52
  576.9 0.0 reduce-scatter.5.cloned.1.call-update
  576.9 0.0 copy-done
  576.9 3.1 bitcast_multiply_fusion
  580.0 2.8 copy.8
  582.8 33.3 %reduce-scatter.5.cloned.1.call-done = f32[80,640]{1,0:T(8,128)} async-done(((f32[640,640]{1,0:T(8,128)}), f32[80,640]{1,0:T(8,128)}) %reduce-scatter.5.cloned.1.call-update) | async-done | bytes 204816 | tf_op jit(solution)/shard_map/reduce_scatter | solution.py:59
  616.2 0.0 copy-done.3
  616.2 1.7 select_multiply_fusion
  (3 shorter events, 0.0 us)
Async XLA Ops:
  7.2 379.7 %all-reduce.3.cloned.1.call-start = ((), (), s32[]{:S(2)}) async-start(), calls=%async_computation.4 | async-start | bytes 31457280 | tf_op jit(solution)/shard_map/psum | solution.py:12
  15.0 47.9 %collective-permute-start = (f32[768,640]{0,1:T(8,128)S(1)}, f32[768,640]{0,1:T(8,128)S(1)}, u32[]{:S(2)}, u32[]{:S(2)}) collective-permute-start(f32[768,640]{0,1:T(8,128)S(1)} %get-tuple-element.8), channel_id=1, source_target_pairs={{0,1},{1,2},{2,3},{3,0},{4,5},{5,6},{6,7},{7,4},{8,9},{9,10},{10,1... | collective-permute-start | bytes 5898248 | tf_op jit(solution)/shard_map/ppermute | solution.py:34
  62.9 1.3 copy-start.1
  64.2 45.9 %collective-permute-start.1 = (f32[768,640]{0,1:T(8,128)S(1)}, f32[768,640]{0,1:T(8,128)}, u32[]{:S(2)}, u32[]{:S(2)}) collective-permute-start(f32[768,640]{0,1:T(8,128)S(1)} %collective-permute-done), channel_id=1, source_target_pairs={{0,1},{1,2},{2,3},{3,0},{4,5},{5,6},{6,7},{7,4},{8,9},{9,10},{10,1... | collective-permute-start | bytes 5898248 | tf_op jit(solution)/shard_map/ppermute | solution.py:34
  110.0 45.2 %collective-permute-start.2 = (f32[768,640]{0,1:T(8,128)}, f32[768,640]{0,1:T(8,128)}, u32[]{:S(2)}, u32[]{:S(2)}) collective-permute-start(f32[768,640]{0,1:T(8,128)} %collective-permute-done.1), channel_id=1, source_target_pairs={{0,1},{1,2},{2,3},{3,0},{4,5},{5,6},{6,7},{7,4},{8,9},{9,10},{10,1... | collective-permute-start | bytes 5898248 | tf_op jit(solution)/shard_map/ppermute | solution.py:34
  110.0 51.2 %copy-start.2 = (f32[768,640]{0,1:T(8,128)S(1)}, f32[768,640]{0,1:T(8,128)}, u32[]{:S(2)}) copy-start(f32[768,640]{0,1:T(8,128)} %copy-done.1) | copy-start | bytes 5898244
  182.7 386.0 %reduce-scatter.3.cloned.1.call-start = ((), (), s32[]{:S(2)}) async-start(), calls=%async_computation.2 | async-start | bytes 9830400 | tf_op jit(solution)/shard_map/reduce_scatter | solution.py:48
  432.0 144.9 %copy-start = (f32[640,768]{1,0:T(8,128)S(1)}, f32[640,768]{1,0:T(8,128)}, u32[]{:S(2)}) copy-start(f32[640,768]{1,0:T(8,128)} %get-tuple-element.9) | copy-start | bytes 5898244
  432.1 184.1 %reduce-scatter.5.cloned.1.call-start = ((), (), s32[]{:S(2)}) async-start(), calls=%async_computation.3 | async-start | bytes 1843200 | tf_op jit(solution)/shard_map/reduce_scatter | solution.py:59
  432.3 183.8 %copy-start.3 = (f32[80,640]{1,0:T(8,128)S(1)}, f32[80,640]{1,0:T(8,128)}, u32[]{:S(2)}) copy-start(f32[80,640]{1,0:T(8,128)} %param.7) | copy-start | bytes 614404
Sparse Core Ops, SparseCore 0:
  182.8 204.0 all-reduce.2
  432.2 136.4 reduce-scatter.2
  577.0 39.1 reduce-scatter.4
